TPU v7x, 32 devices: a whole 2x2x4 slice. The times are simulated.
32 devices in a mesh: seq: 16 (over z, y, x), head: 2 (over core).
Axes of the slice: x: 2, y: 2, z: 4, core: 2. Of those that a mesh axis runs over, the one named last changes fastest.
Arguments:
- queries: bfloat16 [8192, 2048], P('seq', 'head'), may hold values from -37.123106012293746 to 37.123106012293746
- keys: bfloat16 [8192, 2048], P('seq', 'head'), may hold values from -6 to 6
- values: bfloat16 [8192, 2048], P('seq', 'head'), may hold values from -24 to 24
- rand_blocks: int32 [128, 16], P('seq', 'head'), may hold values from 0 to 127, as said below
- global_blocks: int32 [2], replicated, may hold values from 0 to 127
- out_weight: bfloat16 [2048, 4096], P(('head', 'seq')), may hold values from -0.125 to 0.125
Outputs:
- layer_out: bfloat16 [8192, 4096], P(('seq', 'head'))
Inputs may be any that keep to these rules, and one draw needn't show every extreme that they name: `rand_blocks`: of the 8 x 8 entries of one device, at most 8 name blocks of one and the same index of seq (block id // 8), and some index of seq is named exactly 8 times by them.
All inputs are finite; a program needn't handle non-finite values.
Results may differ from a plain program's by a relative error of at most 0.013.
Values may be sent and summed in bfloat16 or wider, within the bound.
A program may use at most 128 MiB of HBM per device.

v0:
```python
import functools

import jax
import jax.numpy as jnp
from jax import lax
from jax.experimental import pallas as pl
from jax.experimental.pallas import tpu as pltpu
from jax.sharding import PartitionSpec as P


def ranked(owners):
    count = owners.shape[0]
    order = jnp.arange(count, dtype=jnp.int32)
    earlier = (owners[:, None] == owners[None, :]) & (order[None, :] < order[:, None])
    return jnp.sum(earlier.astype(jnp.int32), axis=1)


def pack_kernel(cap, block_len, head_dim, head_count, codes_ref, k_ref, v_ref, o_ref):
    dst = pl.program_id(0)
    for s in range(cap):
        code = codes_ref[dst * cap + s]
        row = pl.multiple_of(code // head_count * block_len, block_len)
        col = pl.multiple_of(code % head_count * head_dim, head_dim)
        rows = pl.ds(s * block_len, block_len)
        o_ref[0, rows, 0:head_dim] = k_ref[pl.ds(row, block_len), pl.ds(col, head_dim)]
        o_ref[0, rows, head_dim : 2 * head_dim] = v_ref[pl.ds(row, block_len), pl.ds(col, head_dim)]


def pack(codes, keys, values, n, cap, block_len, head_dim, head_count):
    rows, width = cap * block_len, 2 * head_dim
    whole = lambda d, c: (0, 0)
    return pl.pallas_call(
        functools.partial(pack_kernel, cap, block_len, head_dim, head_count),
        out_shape=jax.ShapeDtypeStruct((n, rows, width), keys.dtype),
        grid_spec=pltpu.PrefetchScalarGridSpec(
            num_scalar_prefetch=1,
            grid=(n,),
            in_specs=[
                pl.BlockSpec(keys.shape, whole),
                pl.BlockSpec(values.shape, whole),
            ],
            out_specs=pl.BlockSpec((1, rows, width), lambda d, c: (d, 0, 0)),
        ),
        cost_estimate=pl.CostEstimate(
            flops=0, transcendentals=0, bytes_accessed=2 * n * rows * width * 2
        ),
        name="pack",
    )(codes, keys, values)


def attend_kernel(
    blocks, block_len, head_dim, head_count, scale,
    own_ref, rank_ref, q_ref, k_ref, v_ref, low_ref, high_ref, kg_ref, vg_ref, arr_ref, o_ref,
):
    h = pl.program_id(0)
    kk = jnp.concatenate([low_ref[0], k_ref[...], high_ref[0]], axis=0)
    vv = jnp.concatenate([low_ref[1], v_ref[...], high_ref[1]], axis=0)
    kg, vg = kg_ref[...], vg_ref[...]
    for b in range(blocks):
        e = b * head_count + h
        owner = own_ref[e]
        rows = pl.ds(pl.multiple_of(rank_ref[e] * block_len, block_len), block_len)
        kr = arr_ref[owner, rows, 0:head_dim]
        vr = arr_ref[owner, rows, head_dim : 2 * head_dim]
        lo, hi = b * block_len, (b + 3) * block_len
        ks = jnp.concatenate([kk[lo:hi], kg, kr], axis=0)
        vs = jnp.concatenate([vv[lo:hi], vg, vr], axis=0)
        q = q_ref[lo : lo + block_len, :]
        s = lax.dot_general(
            q, ks, (((1,), (1,)), ((), ())), preferred_element_type=jnp.float32
        ) * scale
        top = jnp.max(s, axis=-1, keepdims=True)
        expo = jnp.exp(s - top)
        total = jnp.sum(expo, axis=-1, keepdims=True)
        w = (expo * (1.0 / total)).astype(jnp.bfloat16)
        o = jnp.dot(w, vs, preferred_element_type=jnp.float32)
        o_ref[lo : lo + block_len, :] = o.astype(o_ref.dtype)


def attend(owners, ranks, q, k, v, low, high, kg, vg, arrived, blocks, block_len, head_dim, head_count):
    tokens, width = q.shape
    col = lambda h, a, b: (0, h)
    edge = pl.BlockSpec((2, block_len, head_dim), lambda h, a, b: (0, 0, h))
    main = pl.BlockSpec((tokens, head_dim), col)
    glob = pl.BlockSpec((kg.shape[0], head_dim), col)
    return pl.pallas_call(
        functools.partial(
            attend_kernel, blocks, block_len, head_dim, head_count, head_dim ** (-0.5)
        ),
        out_shape=jax.ShapeDtypeStruct(q.shape, jnp.bfloat16),
        grid_spec=pltpu.PrefetchScalarGridSpec(
            num_scalar_prefetch=2,
            grid=(head_count,),
            in_specs=[
                main, main, main, edge, edge, glob, glob,
                pl.BlockSpec(arrived.shape, lambda h, a, b: (0, 0, 0)),
            ],
            out_specs=main,
        ),
        cost_estimate=pl.CostEstimate(
            flops=4 * tokens * 6 * block_len * width,
            transcendentals=tokens * 6 * block_len * head_count,
            bytes_accessed=2 * (4 * q.size + arrived.size),
        ),
        name="attend",
    )(owners, ranks, q, k, v, low, high, kg, vg, arrived)


MESH = pl.DeviceIdType.MESH


def exchange_kernel(
    n, source_ref, w_ref, piece_ref, first_ref, last_ref, full_ref, shared_ref, low_ref, high_ref,
    landed, chosen, line_send, line_recv, near_send, near_recv, far_send, far_recv,
    cut_send, cut_recv, give_send, give_recv, edge_send, edge_recv, local,
):
    lines = n // 4
    me = lax.axis_index("seq")
    z, y, x = me // 4, me // 2 % 2, me % 2
    other_y = z * 4 + (1 - y) * 2 + x
    other_x = z * 4 + y * 2 + 1 - x
    half = w_ref.shape[1] // 2

    barrier = pltpu.get_barrier_semaphore()
    for k in range(1, n):
        pl.semaphore_signal(
            barrier, inc=1, device_id={"seq": lax.rem(me + k, n)}, device_id_type=MESH
        )
    pl.semaphore_wait(barrier, n - 1)

    def remote(src, dst, send, recv, target):
        return pltpu.make_async_remote_copy(
            src_ref=src, dst_ref=dst, send_sem=send, recv_sem=recv,
            device_id={"seq": target}, device_id_type=MESH,
        )

    def origin(side, t):
        return (z - t if side == 0 else z + t) * 4

    def exists(side, t):
        return z - t >= 0 if side == 0 else z + t < lines

    def held(side, t):
        return w_ref if t == 0 else full_ref.at[origin(side, t) + y * 2 + x]

    def along(side, t):
        target = me + 4 if side == 0 else me - 4
        index = origin(side, t) + y * 2 + x
        return remote(
            held(side, t), full_ref.at[index], line_send.at[side, t], line_recv.at[side, t], target
        )

    def passes(side, t):
        ahead = z + 1 < lines if side == 0 else z >= 1
        return jnp.logical_and(exists(side, t), ahead)

    def near(side, t, way):
        index = origin(side, t) + y * 2 + x
        return remote(
            held(side, t), full_ref.at[index], near_send.at[side, t, way],
            near_recv.at[side, t, way], other_y if way == 0 else other_x,
        )

    def far(side, t, way):
        index = origin(side, t) + (
            (1 - y) * 2 + x if way == 0 else y * 2 + 1 - x
        )
        cols = pl.ds(way * half, half)
        return remote(
            full_ref.at[index, :, cols], full_ref.at[index, :, cols], far_send.at[side, t, way],
            far_recv.at[side, t, way], other_x if way == 0 else other_y,
        )

    def sides(t):
        return (0,) if t == 0 else (0, 1)

    def advance(t):
        for side in (0, 1):
            if t > 0:
                @pl.when(exists(side, t))
                def _():
                    along(side, t - 1).wait_recv()
            if t < lines - 1:
                @pl.when(passes(side, t))
                def _():
                    along(side, t).start()
        for side in sides(t):
            @pl.when(exists(side, t))
            def _():
                near(side, t, 0).start()
                near(side, t, 1).start()

    def forward(t):
        for side in sides(t):
            @pl.when(exists(side, t))
            def _():
                for way in (0, 1):
                    near(side, t, way).wait_recv()
                    far(side, t, way).start()

    def cut(k):
        target = lax.rem(me + k, n)
        return remote(
            piece_ref.at[target], landed.at[me], cut_send.at[k], cut_recv.at[k], target
        )

    def give(k):
        target = lax.rem(me + k, n)
        return remote(chosen, shared_ref.at[me], give_send.at[k], give_recv.at[k], target)

    low = remote(last_ref, low_ref, edge_send.at[0], edge_recv.at[0], lax.rem(me + 1, n))
    high = remote(first_ref, high_ref, edge_send.at[1], edge_recv.at[1], lax.rem(me + n - 1, n))
    own_cut = pltpu.make_async_copy(piece_ref.at[me], landed.at[me], local.at[0])
    own_rows = pltpu.make_async_copy(w_ref, full_ref.at[me], local.at[1])
    own_give = pltpu.make_async_copy(chosen, shared_ref.at[me], local.at[2])

    for k in range(1, n):
        cut(k).start()
    own_cut.start()
    own_rows.start()
    advance(0)
    low.start()
    high.start()
    for k in range(1, n):
        cut(k).wait_recv()
    own_cut.wait()
    chosen[...] = landed[source_ref[0]]
    for t in range(1, lines):
        advance(t)
        if t == 1:
            for k in range(1, n):
                give(k).start()
            own_give.start()
        forward(t - 1)
    forward(lines - 1)

    for t in range(lines):
        for side in (0, 1):
            if t < lines - 1:
                @pl.when(passes(side, t))
                def _():
                    along(side, t).wait_send()
        for side in sides(t):
            @pl.when(exists(side, t))
            def _():
                for way in (0, 1):
                    near(side, t, way).wait_send()
                    far(side, t, way).wait()
    for k in range(1, n):
        cut(k).wait_send()
        give(k).wait()
    own_give.wait()
    own_rows.wait()
    low.wait()
    high.wait()


def exchange(source, weight, pieces, first, last, n):
    lines = n // 4
    rows, columns = weight.shape
    dma = pltpu.SemaphoreType.DMA
    vmem = pl.BlockSpec(memory_space=pltpu.VMEM)
    hbm = pl.BlockSpec(memory_space=pl.ANY)
    kind = weight.dtype
    return pl.pallas_call(
        functools.partial(exchange_kernel, n),
        out_shape=(
            jax.ShapeDtypeStruct((n, rows, columns), kind),
            jax.ShapeDtypeStruct(pieces.shape, kind),
            jax.ShapeDtypeStruct(first.shape, kind),
            jax.ShapeDtypeStruct(first.shape, kind),
        ),
        in_specs=[pl.BlockSpec(memory_space=pltpu.SMEM), vmem, vmem, vmem, vmem],
        out_specs=(hbm, hbm, hbm, hbm),
        scratch_shapes=[
            pltpu.VMEM(pieces.shape, kind),
            pltpu.VMEM(pieces.shape[1:], kind),
            dma((2, lines)), dma((2, lines)),
            dma((2, lines, 2)), dma((2, lines, 2)),
            dma((2, lines, 2)), dma((2, lines, 2)),
            dma((n,)), dma((n,)), dma((n,)), dma((n,)),
            dma((2,)), dma((2,)), dma((3,)),
        ],
        compiler_params=pltpu.CompilerParams(collective_id=0, has_side_effects=True),
        cost_estimate=pl.CostEstimate(
            flops=0, transcendentals=0, bytes_accessed=40 * n * rows * columns
        ),
        name="exchange",
    )(source, weight, pieces, first, last)


def body(queries, keys, values, rand_blocks, global_blocks, out_weight):
    f32 = jnp.float32
    n = lax.axis_size("seq")
    block_count, head_count = rand_blocks.shape
    tokens, width = queries.shape
    block_len = tokens // block_count
    head_dim = width // head_count
    entries = block_count * head_count
    cap = max(2, (2 * entries + n - 1) // n)
    g = global_blocks.shape[0]
    wide = 2 * head_dim

    flat_blocks = rand_blocks.reshape(entries)
    owners = flat_blocks // block_count
    head_iota = jnp.arange(entries, dtype=jnp.int32) % head_count
    codes = flat_blocks % block_count * head_count + head_iota
    ranks = ranked(owners)
    slots = owners * cap + ranks
    hits = slots[:, None] == jnp.arange(n * cap, dtype=jnp.int32)[None, :]
    outgoing = jnp.sum(jnp.where(hits, codes[:, None], 0), axis=0).reshape(n, cap)
    incoming = lax.all_to_all(outgoing, "seq", split_axis=0, concat_axis=0, tiled=True)
    wanted = incoming.reshape(n * cap)

    holders = global_blocks // block_count
    offsets = global_blocks % block_count * block_len
    share = n // g
    thin = block_len * width // (share * head_dim)

    def cut(array, member):
        piece = lax.dynamic_slice_in_dim(array, offsets[member], block_len, 0)
        return piece.reshape(share, thin // 2, wide)

    pieces = jnp.concatenate(
        [jnp.concatenate([cut(keys, m), cut(values, m)], axis=1) for m in range(g)], axis=0
    )
    packed = pack(wanted, keys, values, n, cap, block_len, head_dim, head_count)
    arrived = lax.all_to_all(packed, "seq", split_axis=0, concat_axis=0, tiled=True)
    source = holders[lax.axis_index("seq") // share].reshape(1)
    first = jnp.stack([keys[:block_len], values[:block_len]])
    last = jnp.stack([keys[-block_len:], values[-block_len:]])
    weight, packed = lax.optimization_barrier((out_weight, packed))
    group_rows, shared, low, high = exchange(source, weight, pieces, first, last, n)
    group_rows = group_rows.reshape(n * out_weight.shape[0], out_weight.shape[1])
    kg = shared[:, : thin // 2].reshape(g * block_len, width)
    vg = shared[:, thin // 2 :].reshape(g * block_len, width)

    attended = attend(
        owners, ranks, queries, keys, values, low, high, kg, vg, arrived,
        block_count, block_len, head_dim, head_count,
    )
    partial_value = jnp.dot(attended, group_rows, preferred_element_type=f32)
    return lax.psum_scatter(
        partial_value.astype(jnp.bfloat16), "head", scatter_dimension=0, tiled=True
    )


def solution(mesh):
    placed = (
        P("seq", "head"),
        P("seq", "head"),
        P("seq", "head"),
        P("seq", "head"),
        P(),
        P(("head", "seq"), None),
    )
    return jax.shard_map(
        body, mesh=mesh, in_specs=placed, out_specs=P(("seq", "head"), None), check_vma=False
    )
```

profile of v0, /device:TPU:0, one launch (start us, length us, event | category | flops | bytes accessed | tf_op | source)
XLA Modules:
  0.0 281.9 jit_solution(11242610836070595823)
XLA Ops:
  6.5 0.0 copy-start.1
  6.5 0.0 copy-start
  6.5 0.0 copy-start.4
  6.5 0.9 reshape.133
  7.5 0.0 copy-start.2
  7.5 0.2 convert_reduce_fusion.rank_ref
  7.7 0.0 copy-start.3
  7.7 0.1 select_reduce_fusion
  7.8 0.1 all_to_all.9
  7.9 15.4 %all_to_all.14 = s32[16,1,8]{2,1,0:T(1,128)S(1)} all-to-all(s32[16,1,8]{2,1,0:T(1,128)S(1)} %bitcast.14), channel_id=1, replica_groups=mesh['seq'=16,'head'=2] {'seq'}, dimensions={0} | all-to-all | bytes 1024 | tf_op jit(solution)/shard_map/all_to_all | solution.py:312
  23.3 0.5 broadcast.178
  23.8 0.7 reduce.3
  24.4 0.6 reshape.134.codes_ref
  25.1 8.5 %pack.1 = bf16[16,512,256]{2,1,0:T(8,128)(2,1)} custom-call(s32[128]{0:T(128)} %reshape.134.codes_ref, bf16[512,1024]{1,0:T(8,128)(2,1)} %k_ref.3, bf16[512,1024]{1,0:T(8,128)(2,1)} %v_ref.3), custom_call_target="tpu_custom_call" | custom-call | bytes 8388608 | tf_op jit(solution)/shard_map/pack/pallas_call | solution.py:32
  33.6 4.6 %all-to-all-start.1 = ((bf16[16,512,256]{2,1,0:T(8,128)(2,1)}), bf16[16,512,256]{2,1,0:T(8,128)(2,1)}, u32[]{:S(2)}, u32[]{:S(2)}) async-start(bf16[16,512,256]{2,1,0:T(8,128)(2,1)} %pack.1), calls=%async_computation.1 | async-start | bytes 8388608 | tf_op jit(solution)/shard_map/all_to_all | solution.py:328
  38.2 0.0 reduce-scatter.2.cloned.1.call-start
  38.2 0.0 copy-done.4
  38.3 0.6 fusion.5
  42.6 0.0 copy-done.1
  42.7 0.0 copy-done
  42.7 0.2 slice_bitcast_fusion
  42.8 0.0 copy-done.2
  42.9 0.0 copy-done.3
  42.9 0.1 reshape.138
  43.0 0.1 reshape.136
  43.1 0.1 reshape.135
  43.2 0.1 reshape.137
  43.3 0.6 dynamic_slice.15.source_ref
  43.9 0.7 pad_maximum_fusion.1.last_ref
  44.6 0.7 pad_maximum_fusion.first_ref
  45.3 0.8 maximum_maximum_fusion.piece_ref
  46.2 170.8 %exchange.1 = (bf16[16,64,4096]{2,1,0:T(8,128)(2,1)}, bf16[16,64,256]{2,1,0:T(8,128)(2,1)}, bf16[2,64,1024]{2,1,0:T(8,128)(2,1)}, bf16[2,64,1024]{2,1,0:T(8,128)(2,1)}) custom-call(s32[1]{0:T(128)} %dynamic_slice.15.source_ref, bf16[64,4096]{1,0:T(8,128)(2,1)} %w_ref, bf16[16,64,256]{2,1,0:T(8,128)(2,1)} %maximum_maximum_fusion.piece_ref, ...), custom_call_target="tpu_custom_call" | custom-call | bytes 167772160 | tf_op jit(solution)/shard_map/exchange/pallas_call | solution.py:265
  217.0 1.1 fusion.4
  218.1 0.9 reshape.140.vg_ref
  218.9 0.9 reshape.139.kg_ref
  219.8 0.0 all-to-all-done.1.arr_ref
  219.8 26.6 %attend.1 = bf16[512,1024]{1,0:T(8,128)(2,1)} custom-call(s32[64]{0:T(128)} %copy-done.2, s32[64]{0:T(128)} %copy-done.3, bf16[512,1024]{1,0:T(8,128)(2,1)} %q_ref.1, bf16[512,1024]{1,0:T(8,128)(2,1)} %k_ref.3, bf16[512,1024]{1,0:T(8,128)(2,1)} %v_ref.3, bf16[2,64,1024]{2,1,0:T(8,128)(2,1)} %get-tuple-element.11.low_ref, ...), custom_call_target="tpu_custom_call" | custom-call | flops 805306368 | bytes 8388608 | tf_op jit(solution)/shard_map/attend/pallas_call | solution.py:86
  246.4 10.2 %convolution_convert_fusion = bf16[512,4096]{1,0:T(8,128)(2,1)} fusion(bf16[512,1024]{1,0:T(8,128)(2,1)} %attend.1, bf16[1024,4096]{1,0:T(8,128)(2,1)} %bitcast.15), kind=kOutput, calls=%fused_computation | convolution fusion | flops 4297064448 | bytes 13631488 | tf_op jit(solution)/shard_map/dot_general | solution.py:342
  256.6 0.0 reduce-scatter.2.cloned.1.call-update
  256.6 18.4 %reduce-scatter.2.cloned.1.call-done = bf16[256,4096]{1,0:T(8,128)(2,1)} async-done(((bf16[512,4096]{1,0:T(8,128)(2,1)}), bf16[256,4096]{1,0:T(8,128)(2,1)}) %reduce-scatter.2.cloned.1.call-update) | async-done | bytes 2097168 | tf_op jit(solution)/shard_map/reduce_scatter | solution.py:343
  (3 shorter events, 0.0 us)
Async XLA Ops:
  6.5 36.1 %copy-start.1 = (bf16[512,1024]{1,0:T(8,128)(2,1)S(1)}, bf16[512,1024]{1,0:T(8,128)(2,1)}, u32[]{:S(2)}) copy-start(bf16[512,1024]{1,0:T(8,128)(2,1)} %v_ref.3) | copy-start | bytes 3145732
  6.5 36.1 %copy-start = (bf16[512,1024]{1,0:T(8,128)(2,1)S(1)}, bf16[512,1024]{1,0:T(8,128)(2,1)}, u32[]{:S(2)}) copy-start(bf16[512,1024]{1,0:T(8,128)(2,1)} %k_ref.3) | copy-start | bytes 3145732
  6.5 31.7 %copy-start.4 = (s32[2]{0:T(128)S(1)}, s32[2]{0:T(128)}, u32[]{:S(2)}) copy-start(s32[2]{0:T(128)} %param.10) | copy-start | bytes 28
  7.5 35.4 %copy-start.2 = (s32[64]{0:T(128)}, s32[64]{0:T(128)S(1)}, u32[]{:S(2)}) copy-start(s32[64]{0:T(128)S(1)} %get-tuple-element.30.own_ref) | copy-start | bytes 772
  7.7 35.2 %copy-start.3 = (s32[64]{0:T(128)}, s32[64]{0:T(128)S(1)}, u32[]{:S(2)}) copy-start(s32[64]{0:T(128)S(1)} %convert_reduce_fusion.rank_ref) | copy-start | bytes 772
  33.6 186.2 %all-to-all-start.1 = ((bf16[16,512,256]{2,1,0:T(8,128)(2,1)}), bf16[16,512,256]{2,1,0:T(8,128)(2,1)}, u32[]{:S(2)}, u32[]{:S(2)}) async-start(bf16[16,512,256]{2,1,0:T(8,128)(2,1)} %pack.1), calls=%async_computation.1 | async-start | bytes 8388608 | tf_op jit(solution)/shard_map/all_to_all | solution.py:328
  38.2 236.8 %reduce-scatter.2.cloned.1.call-start = ((), (), s32[]{:S(2)}) async-start(), calls=%async_computation.3 | async-start | bytes 6291456 | tf_op jit(solution)/shard_map/reduce_scatter | solution.py:343
Sparse Core Ops, SparseCore 0:
  256.7 18.2 reduce-scatter.1
where the time goes:
time: 282 us
  Pallas kernels  206 us (73%)
  waiting for transfers between devices  18.5 us (7%)
  between operations  17.3 us (6%)
  blocking collectives  15.4 us (5%)
  matrix products  10.2 us (4%)
  local copies, waits for them, and re-layouts  6.68 us (2%)
  starting transfers between devices  4.6 us (2%)
  other arithmetic  3.27 us (1%)
    pallas_call x1, Pallas kernels, exchange(): pl.pallas_call(functools.partial(exchange_kernel, n), out_shape=(jax.Shap...  171 us
    pallas_call x1, Pallas kernels, attend(): pl.pallas_call(functools.partial(attend_kernel, blocks, block_len, head_d...  26.6 us
    reduce_scatter x1, waiting for transfers between devices, body(): lax.psum_scatter(partial_value.astype(jnp.bfloat16), 'head', scatter_dime...  18.4 us
    all_to_all x1, blocking collectives, body(): lax.all_to_all(outgoing, 'seq', split_axis=0, concat_axis=0, tiled=True)  15.4 us
    dot_general x1, matrix products, body(): partial_value = jnp.dot(attended, group_rows, preferred_element_type=f32)  10.2 us
    pallas_call x1, Pallas kernels, pack(): pl.pallas_call(functools.partial(pack_kernel, cap, block_len, head_dim, h...  8.55 us
  transfers between devices with their start and end apart: 2, of which 1 were waited for; matrix products, arithmetic and copies ran while one was open for 2% of the time, Pallas kernels for 61%

commit v1 on v0

v1 whole, which is shorter than its diff:
```python
import functools

import jax
import jax.numpy as jnp
from jax import lax
from jax.experimental import pallas as pl
from jax.experimental.pallas import tpu as pltpu
from jax.sharding import PartitionSpec as P

MESH = pl.DeviceIdType.MESH
LANES = 128
TILE = 16


def ranked(owners):
    count = owners.shape[0]
    order = jnp.arange(count, dtype=jnp.int32)
    earlier = (owners[:, None] == owners[None, :]) & (order[None, :] < order[:, None])
    return jnp.sum(earlier.astype(jnp.int32), axis=1)


def layer_kernel(
    n, cap, blocks, block_len, head_dim, heads, scale,
    glob_ref, slot_ref, codes_ref, q_ref, k_ref, v_ref, w_ref,
    full_ref, o_ref,
    pairs, stage, arr, codes_in, codes, low, high, pair_x, send_x, pair_y, send_y, cut_z, got_z, shared,
    acc, top_s, sum_s,
    line_send, line_recv, near_send, near_recv, far_send, far_recv,
    code_send, code_recv, rand_send, rand_recv, edge_send, edge_recv,
    glob_send, glob_recv, zcut_send, zcut_recv, zgive_send, zgive_recv, local,
):
    lines = n // 4
    me = lax.axis_index("seq")
    z, y, x = me // 4, me // 2 % 2, me % 2
    other_y = z * 4 + (1 - y) * 2 + x
    other_x = z * 4 + y * 2 + 1 - x
    half = w_ref.shape[1] // 2
    tiles = block_len // TILE
    share = heads * tiles // lines
    wide = 2 * head_dim

    barrier = pltpu.get_barrier_semaphore()

    def greet(k, c):
        pl.semaphore_signal(
            barrier, inc=1, device_id={"seq": lax.rem(me + k, n)}, device_id_type=MESH
        )
        return c

    lax.fori_loop(1, n, greet, 0)
    pl.semaphore_wait(barrier, n - 1)

    def remote(src, dst, send, recv, target):
        return pltpu.make_async_remote_copy(
            src_ref=src, dst_ref=dst, send_sem=send, recv_sem=recv,
            device_id={"seq": target}, device_id_type=MESH,
        )

    def origin(side, t):
        return (z - t if side == 0 else z + t) * 4

    def exists(side, t):
        return z - t >= 0 if side == 0 else z + t < lines

    def held(side, t):
        return w_ref if t == 0 else full_ref.at[origin(side, t) + y * 2 + x]

    def along(side, t):
        target = me + 4 if side == 0 else me - 4
        index = origin(side, t) + y * 2 + x
        return remote(
            held(side, t), full_ref.at[index], line_send.at[side, t], line_recv.at[side, t], target
        )

    def passes(side, t):
        ahead = z + 1 < lines if side == 0 else z >= 1
        return jnp.logical_and(exists(side, t), ahead)

    def near(side, t, way):
        index = origin(side, t) + y * 2 + x
        return remote(
            held(side, t), full_ref.at[index], near_send.at[side, t, way],
            near_recv.at[side, t, way], other_y if way == 0 else other_x,
        )

    def far(side, t, way):
        index = origin(side, t) + (
            (1 - y) * 2 + x if way == 0 else y * 2 + 1 - x
        )
        cols = pl.ds(way * half, half)
        return remote(
            full_ref.at[index, :, cols], full_ref.at[index, :, cols], far_send.at[side, t, way],
            far_recv.at[side, t, way], other_x if way == 0 else other_y,
        )

    def sides(t):
        return (0,) if t == 0 else (0, 1)

    def advance(t):
        for side in (0, 1):
            if t > 0:
                @pl.when(exists(side, t))
                def _():
                    along(side, t - 1).wait_recv()
            if t < lines - 1:
                @pl.when(passes(side, t))
                def _():
                    along(side, t).start()
        for side in sides(t):
            @pl.when(exists(side, t))
            def _():
                near(side, t, 0).start()
                near(side, t, 1).start()

    def forward(t):
        for side in sides(t):
            @pl.when(exists(side, t))
            def _():
                for way in (0, 1):
                    near(side, t, way).wait_recv()
                    far(side, t, way).start()

    def code(k):
        target = lax.rem(me + k, n)
        return remote(
            codes_ref.at[target], codes_in.at[me], code_send.at[k], code_recv.at[k], target
        )

    def rand(k):
        target = lax.rem(me + k, n)
        return remote(
            stage.at[pl.ds(target * cap, cap)], arr.at[pl.ds(me * cap, cap)],
            rand_send.at[k], rand_recv.at[k], target,
        )

    def each(body):
        def step(k, c):
            body(k)
            return c
        lax.fori_loop(1, n, step, 0)

    each(lambda k: code(k).start())
    codes_in[pl.ds(me, 1)] = codes_ref[pl.ds(me, 1)]

    own_rows = pltpu.make_async_copy(w_ref, full_ref.at[me], local.at[0])
    own_rows.start()
    advance(0)

    tail = (blocks - 1) * block_len
    up, down = lax.rem(me + 1, n), lax.rem(me + n - 1, n)
    edges = []
    for i, ref in enumerate((k_ref, v_ref)):
        edges.append(remote(
            ref.at[tail : tail + block_len], low.at[i], edge_send.at[0, i], edge_recv.at[0, i], up
        ))
        edges.append(remote(
            ref.at[0:block_len], high.at[i], edge_send.at[1, i], edge_recv.at[1, i], down
        ))
    for copy in edges:
        copy.start()

    for b in range(blocks):
        rows = slice(b * block_len, (b + 1) * block_len)
        for h in range(heads):
            cols = slice(h * head_dim, (h + 1) * head_dim)
            pairs[b * heads + h, :, 0:head_dim] = k_ref[rows, cols]
            pairs[b * heads + h, :, head_dim:wide] = v_ref[rows, cols]

    def candidate(block, out, lead):
        for h in range(heads):
            pair = pairs[block % blocks * heads + h]
            for r in range(tiles):
                rows = slice(r * TILE, (r + 1) * TILE)
                out[(*lead, 0, h * tiles + r)] = pair[rows, 0:head_dim]
                out[(*lead, 1, h * tiles + r)] = pair[rows, head_dim:wide]

    away = glob_ref[1 - x]
    candidate(away, send_x, ())
    glob_x = remote(send_x, pair_x.at[1], glob_send.at[0], glob_recv.at[0], other_x)
    glob_x.start()
    mine = glob_ref[x]
    candidate(mine, pair_x, (0,))
    holder = mine // blocks
    pick_x = lax.rem(holder + x, 2)
    pick_y = lax.rem(holder // 2 + y, 2)
    pick_z = holder // 4

    each(lambda k: code(k).wait_recv())
    to_smem = pltpu.make_async_copy(codes_in, codes, local.at[1])
    to_smem.start()
    to_smem.wait()

    def pack(target, out, place):
        for s in range(cap):
            out[place * cap + s] = pairs[codes[target, 0, s]]

    def ship(k):
        target = lax.rem(me + k, n)
        pack(target, stage, target)
        rand(k).start()

    each(ship)
    pack(me, arr, me)

    glob_x.wait_recv()
    picked = pair_x.at[:, 1 - y]
    send_y[...] = picked[pick_x]
    glob_y = remote(send_y, pair_y.at[1], glob_send.at[1], glob_recv.at[1], other_y)
    glob_y.start()
    picked = pair_x.at[:, y]
    pair_y[0] = picked[pick_x]

    advance(1)

    def line(dz):
        return lax.rem(z + dz, lines)

    def zcut(dz):
        to = line(dz)
        return remote(
            cut_z.at[pl.ds(to * share, share)], got_z.at[z], zcut_send.at[dz], zcut_recv.at[dz],
            to * 4 + y * 2 + x,
        )

    def zgive(dz):
        piece = shared.at[x, y, pl.ds(z * share, share)]
        return remote(
            piece, piece, zgive_send.at[dz], zgive_recv.at[dz], line(dz) * 4 + y * 2 + x
        )

    glob_y.wait_recv()
    cut_z[...] = pair_y[pick_y]
    for dz in range(1, lines):
        zcut(dz).start()
    got_z[z] = cut_z[pl.ds(z * share, share)]

    forward(0)

    for dz in range(1, lines):
        zcut(dz).wait_recv()
    shared[x, y, pl.ds(z * share, share)] = got_z[pick_z]
    for dz in range(1, lines):
        zgive(dz).start()
    for dz in range(1, lines):
        zgive(dz).wait_recv()
    give_y = remote(
        shared.at[x, y], shared.at[x, y], glob_send.at[2], glob_recv.at[2], other_y
    )
    give_y.start()
    give_y.wait_recv()
    give_x = remote(shared.at[x], shared.at[x], glob_send.at[3], glob_recv.at[3], other_x)
    give_x.start()

    if lines > 2:
        advance(2)
    give_x.wait_recv()
    for copy in edges:
        copy.wait_recv()

    def begin(h, c):
        cols = pl.ds(pl.multiple_of(h * head_dim, head_dim), head_dim)
        kk = jnp.concatenate([low[0, :, cols], k_ref[:, cols], high[0, :, cols]], axis=0)
        vv = jnp.concatenate([low[1, :, cols], v_ref[:, cols], high[1, :, cols]], axis=0)
        chunk = pl.ds(h * tiles, tiles)
        kg = [shared[i, 0, chunk].reshape(block_len, head_dim) for i in range(2)]
        vg = [shared[i, 1, chunk].reshape(block_len, head_dim) for i in range(2)]
        for b in range(blocks):
            lo, hi = b * block_len, (b + 3) * block_len
            ks = jnp.concatenate([kk[lo:hi], *kg], axis=0)
            vs = jnp.concatenate([vv[lo:hi], *vg], axis=0)
            s = lax.dot_general(
                q_ref[lo : lo + block_len, cols], ks, (((1,), (1,)), ((), ())),
                preferred_element_type=jnp.float32,
            ) * scale
            top = jnp.max(s, axis=-1, keepdims=True)
            expo = jnp.exp(s - top)
            total = jnp.sum(expo, axis=-1, keepdims=True)
            rows = pl.ds(lo, block_len)
            acc[rows, cols] = jnp.dot(
                expo.astype(jnp.bfloat16), vs, preferred_element_type=jnp.float32
            )
            top_s[h, rows] = jnp.broadcast_to(top, (block_len, LANES))
            sum_s[h, rows] = jnp.broadcast_to(total, (block_len, LANES))
        return c

    def finish(h, c):
        cols = pl.ds(pl.multiple_of(h * head_dim, head_dim), head_dim)
        for b in range(blocks):
            e = b * heads + h
            pair = arr[slot_ref[e]]
            kr, vr = pair[:, 0:head_dim], pair[:, head_dim:wide]
            rows = pl.ds(b * block_len, block_len)
            s = lax.dot_general(
                q_ref[rows, cols], kr, (((1,), (1,)), ((), ())),
                preferred_element_type=jnp.float32,
            ) * scale
            before = top_s[h, rows, 0:1]
            top = jnp.maximum(before, jnp.max(s, axis=-1, keepdims=True))
            fade = jnp.exp(before - top)
            expo = jnp.exp(s - top)
            total = sum_s[h, rows, 0:1] * fade + jnp.sum(expo, axis=-1, keepdims=True)
            o = acc[rows, cols] * fade + jnp.dot(
                expo.astype(jnp.bfloat16), vr, preferred_element_type=jnp.float32
            )
            o_ref[rows, cols] = (o * (1.0 / total)).astype(o_ref.dtype)
        return c

    steps = [functools.partial(forward, 1)]
    for t in range(3, lines):
        steps += [functools.partial(advance, t), functools.partial(forward, t - 1)]
    cutoffs = [heads * i // len(steps) for i in range(len(steps) + 1)]
    for step, h0, h1 in zip(steps, cutoffs, cutoffs[1:]):
        if h1 > h0:
            lax.fori_loop(h0, h1, begin, 0)
        step()
    forward(lines - 1)

    each(lambda k: rand(k).wait_recv())
    lax.fori_loop(0, heads, finish, 0)

    for t in range(lines):
        for side in (0, 1):
            if t < lines - 1:
                @pl.when(passes(side, t))
                def _():
                    along(side, t).wait_send()
        for side in sides(t):
            @pl.when(exists(side, t))
            def _():
                for way in (0, 1):
                    near(side, t, way).wait_send()
                    far(side, t, way).wait()
    each(lambda k: code(k).wait_send())
    each(lambda k: rand(k).wait_send())
    for dz in range(1, lines):
        zcut(dz).wait_send()
        zgive(dz).wait_send()
    for copy in (glob_x, glob_y, give_y, give_x, *edges):
        copy.wait_send()
    own_rows.wait()


def layer(glob, places, codes, q, k, v, weight, n, cap, blocks, block_len, head_dim, heads):
    lines = n // 4
    rows, columns = weight.shape
    tokens, width = q.shape
    tiles = heads * block_len // TILE
    dma = pltpu.SemaphoreType.DMA
    vmem = pl.BlockSpec(memory_space=pltpu.VMEM)
    smem = pl.BlockSpec(memory_space=pltpu.SMEM)
    hbm = pl.BlockSpec(memory_space=pl.ANY)
    kind = q.dtype
    f32 = jnp.float32
    slots = (n * cap, block_len, 2 * head_dim)
    tile = (TILE, LANES)
    return pl.pallas_call(
        functools.partial(
            layer_kernel, n, cap, blocks, block_len, head_dim, heads, head_dim ** (-0.5)
        ),
        out_shape=(
            jax.ShapeDtypeStruct((n, rows, columns), kind),
            jax.ShapeDtypeStruct((tokens, width), kind),
        ),
        in_specs=[smem, smem, vmem, vmem, vmem, vmem, vmem],
        out_specs=(hbm, vmem),
        scratch_shapes=[
            pltpu.VMEM((blocks * heads, block_len, 2 * head_dim), kind),
            pltpu.VMEM(slots, kind),
            pltpu.VMEM(slots, kind),
            pltpu.VMEM(codes.shape, jnp.int32),
            pltpu.SMEM(codes.shape, jnp.int32),
            pltpu.VMEM((2, block_len, width), kind),
            pltpu.VMEM((2, block_len, width), kind),
            pltpu.VMEM((2, 2, tiles, *tile), kind),
            pltpu.VMEM((2, tiles, *tile), kind),
            pltpu.VMEM((2, tiles, *tile), kind),
            pltpu.VMEM((tiles, *tile), kind),
            pltpu.VMEM((tiles, *tile), kind),
            pltpu.VMEM((lines, tiles // lines, *tile), kind),
            pltpu.VMEM((2, 2, tiles, *tile), kind),
            pltpu.VMEM((tokens, width), f32),
            pltpu.VMEM((heads, tokens, LANES), f32),
            pltpu.VMEM((heads, tokens, LANES), f32),
            dma((2, lines)), dma((2, lines)),
            dma((2, lines, 2)), dma((2, lines, 2)),
            dma((2, lines, 2)), dma((2, lines, 2)),
            dma((n,)), dma((n,)), dma((n,)), dma((n,)),
            dma((2, 2)), dma((2, 2)),
            dma((4,)), dma((4,)),
            dma((lines,)), dma((lines,)), dma((lines,)), dma((lines,)),
            dma((2,)),
        ],
        compiler_params=pltpu.CompilerParams(
            collective_id=0, has_side_effects=True, vmem_limit_bytes=48 << 20
        ),
        cost_estimate=pl.CostEstimate(
            flops=4 * tokens * 6 * block_len * width,
            transcendentals=tokens * 6 * block_len * heads,
            bytes_accessed=40 * n * rows * columns,
        ),
        name="layer",
    )(glob, places, codes, q, k, v, weight)


def body(queries, keys, values, rand_blocks, global_blocks, out_weight):
    f32 = jnp.float32
    n = lax.axis_size("seq")
    block_count, head_count = rand_blocks.shape
    tokens, width = queries.shape
    block_len = tokens // block_count
    head_dim = width // head_count
    entries = block_count * head_count
    cap = max(2, (2 * entries + n - 1) // n)

    flat_blocks = rand_blocks.reshape(entries)
    owners = flat_blocks // block_count
    head_iota = jnp.arange(entries, dtype=jnp.int32) % head_count
    codes = flat_blocks % block_count * head_count + head_iota
    ranks = ranked(owners)
    target = jnp.arange(n, dtype=jnp.int32)[:, None, None]
    slot = jnp.arange(LANES, dtype=jnp.int32)[None, :, None]
    hits = (owners[None, None, :] == target) & (ranks[None, None, :] == slot)
    outgoing = jnp.sum(jnp.where(hits, codes[None, None, :], 0), axis=2)

    group_rows, attended = layer(
        global_blocks, owners * cap + ranks, outgoing.reshape(n, 1, LANES), queries, keys, values,
        out_weight, n, cap, block_count, block_len, head_dim, head_count,
    )
    group_rows = group_rows.reshape(n * out_weight.shape[0], out_weight.shape[1])
    partial_value = jnp.dot(attended, group_rows, preferred_element_type=f32)
    return lax.psum_scatter(
        partial_value.astype(jnp.bfloat16), "head", scatter_dimension=0, tiled=True
    )


def solution(mesh):
    placed = (
        P("seq", "head"),
        P("seq", "head"),
        P("seq", "head"),
        P("seq", "head"),
        P(),
        P(("head", "seq"), None),
    )
    return jax.shard_map(
        body, mesh=mesh, in_specs=placed, out_specs=P(("seq", "head"), None), check_vma=False
    )
```

time: 282 us -> 243 us (0.86)
  blocking collectives: 15.4 us -> 0 us
  waiting for transfers between devices: 18.5 us -> 11.1 us
  starting transfers between devices: 4.6 us -> 0.01 us
  Pallas kernels: 206 us -> 202 us
  between operations: 17.3 us -> 13.4 us
    all_to_all x1 -> x0, blocking collectives: 15.4 us -> none  [body(): lax.all_to_all(outgoing, 'seq', split_axis=0, concat_axis=0, tiled=True)]
    reduce_scatter x1, waiting for transfers between devices: 18.4 us -> 11 us  [body(): lax.psum_scatter(partial_value.astype(jnp.bfloat16), 'head', scatter_dime...]
    unnamed x10, local copies, waits for them, and re-layouts: 0.02 us -> 5.36 us
    all_to_all x1 -> x0, starting transfers between devices: 4.56 us -> none  [body(): lax.all_to_all(packed, 'seq', split_axis=0, concat_axis=0, tiled=True)]
    pallas_call x3 -> x1, Pallas kernels: 206 us -> 202 us  [layer(): pl.pallas_call(functools.partial(layer_kernel, n, cap, blocks, block_len,...]
  transfers between devices with their start and end apart: 2 -> 1, of which waited for: 1 -> 1; matrix products, arithmetic and copies ran while one was open for 2% -> 0% of each run, Pallas kernels for 61% -> 0%
where the time goes in v1:
time: 243 us
  Pallas kernels  202 us (83%)
  between operations  13.4 us (6%)
  waiting for transfers between devices  11.1 us (5%)
  matrix products  9.39 us (4%)
  local copies, waits for them, and re-layouts  6.13 us (3%)
    pallas_call x1, Pallas kernels, layer(): pl.pallas_call(functools.partial(layer_kernel, n, cap, blocks, block_len,...  202 us
    reduce_scatter x1, waiting for transfers between devices, body(): lax.psum_scatter(partial_value.astype(jnp.bfloat16), 'head', scatter_dime...  11 us
    dot_general x1, matrix products, body(): partial_value = jnp.dot(attended, group_rows, preferred_element_type=f32)  9.39 us
    unnamed x10, local copies, waits for them, and re-layouts  5.36 us
  transfers between devices with their start and end apart: 1, of which 1 were waited for; matrix products, arithmetic and copies ran while one was open for 0% of the time, Pallas kernels for 0%

profile of v1, /device:TPU:0, one launch (start us, length us, event | category | flops | bytes accessed | tf_op | source)
XLA Modules:
  0.0 242.8 jit_solution(3068319009438321456)
XLA Ops:
  6.5 0.0 reduce-scatter.2.cloned.1.call-start
  6.5 0.8 reshape.172
  7.3 0.2 convert_reduce_fusion
  7.5 0.1 iota_compare_fusion
  7.6 0.2 select_reduce_fusion
  7.8 0.0 copy-start
  7.9 1.2 copy-done
  9.1 0.0 copy-start.1
  9.1 1.2 copy-done.1
  10.3 0.0 copy-start.2
  10.3 1.2 copy-done.2
  11.5 0.0 copy-start.3
  11.5 1.0 copy-done.3
  12.6 0.0 copy-start.4
  12.6 0.7 copy-done.4
  13.2 202.2 %layer.1 = (bf16[16,64,4096]{2,1,0:T(8,128)(2,1)}, bf16[512,1024]{1,0:T(8,128)(2,1)S(1)}) custom-call(s32[2]{0:T(128)S(1)} %copy-done.4, s32[64]{0:T(128)S(1)} %multiply_add_fusion.slot_ref, s32[16,1,128]{2,1,0:T(1,128)S(1)} %bitcast.4, bf16[512,1024]{1,0:T(8,128)(2,1)S(1)} %copy-done, bf16[512,1024]{1,0:T(8,128)(2,1)S(1)} %copy-done.1, ...), custom_call_target="tpu_custom_call" | custom-call | flops 805306368 | bytes 167772160 | tf_op jit(solution)/shard_map/layer/pallas_call | solution.py:356
  215.5 9.4 %convolution_convert_fusion = bf16[512,4096]{1,0:T(8,128)(2,1)} fusion(bf16[512,1024]{1,0:T(8,128)(2,1)S(1)} %get-tuple-element.7, bf16[1024,4096]{1,0:T(8,128)(2,1)} %bitcast.5), kind=kOutput, calls=%fused_computation | convolution fusion | flops 4297064448 | bytes 13631488 | tf_op jit(solution)/shard_map/dot_general | solution.py:430
  224.9 0.0 reduce-scatter.2.cloned.1.call-update
  224.9 11.0 %reduce-scatter.2.cloned.1.call-done = bf16[256,4096]{1,0:T(8,128)(2,1)} async-done(((bf16[512,4096]{1,0:T(8,128)(2,1)}), bf16[256,4096]{1,0:T(8,128)(2,1)}) %reduce-scatter.2.cloned.1.call-update) | async-done | bytes 2097168 | tf_op jit(solution)/shard_map/reduce_scatter | solution.py:431
  (3 shorter events, 0.0 us)
Async XLA Ops:
  6.5 229.4 %reduce-scatter.2.cloned.1.call-start = ((), (), s32[]{:S(2)}) async-start(), calls=%async_computation.1 | async-start | bytes 6291456 | tf_op jit(solution)/shard_map/reduce_scatter | solution.py:431
  7.8 1.2 copy-start
  9.1 1.2 copy-start.1
  10.3 1.2 copy-start.2
  11.5 1.0 copy-start.3
  12.6 0.7 copy-start.4
Sparse Core Ops, SparseCore 0:
  225.0 10.8 reduce-scatter.1

commit v2 on v1

--- a/solution.py
+++ b/solution.py
@@ -9,7 +9,6 @@
 
 MESH = pl.DeviceIdType.MESH
 LANES = 128
-TILE = 16
 
 
 def ranked(owners):
@@ -21,13 +20,14 @@
 
 def layer_kernel(
     n, cap, blocks, block_len, head_dim, heads, scale,
-    glob_ref, slot_ref, codes_ref, q_ref, k_ref, v_ref, w_ref,
-    full_ref, o_ref,
-    pairs, stage, arr, codes_in, codes, low, high, pair_x, send_x, pair_y, send_y, cut_z, got_z, shared,
+    glob_ref, slot_ref, codes_ref, q_hbm, k_hbm, v_hbm, w_ref,
+    out_ref,
+    q_ref, k_ref, v_ref, full_ref, att, give, take,
+    pairs, stage, arr, codes_in, codes, low, high, cand, got_p, got_z, shared,
     acc, top_s, sum_s,
     line_send, line_recv, near_send, near_recv, far_send, far_recv,
     code_send, code_recv, rand_send, rand_recv, edge_send, edge_recv,
-    glob_send, glob_recv, zcut_send, zcut_recv, zgive_send, zgive_recv, local,
+    cut_send, cut_recv, line_out, line_in, give_send, give_recv, core_send, core_recv, local,
 ):
     lines = n // 4
     me = lax.axis_index("seq")
@@ -35,9 +35,16 @@
     other_y = z * 4 + (1 - y) * 2 + x
     other_x = z * 4 + y * 2 + 1 - x
     half = w_ref.shape[1] // 2
-    tiles = block_len // TILE
-    share = heads * tiles // lines
+    part = heads // 2
     wide = 2 * head_dim
+
+    hd = lax.axis_index("head")
+    loads = [
+        pltpu.make_async_copy(src, dst, local.at[2 + i])
+        for i, (src, dst) in enumerate(((k_hbm, k_ref), (v_hbm, v_ref), (q_hbm, q_ref)))
+    ]
+    for copy in loads:
+        copy.start()
 
     barrier = pltpu.get_barrier_semaphore()
 
@@ -48,7 +55,8 @@
         return c
 
     lax.fori_loop(1, n, greet, 0)
-    pl.semaphore_wait(barrier, n - 1)
+    pl.semaphore_signal(barrier, inc=1, device_id={"head": 1 - hd}, device_id_type=MESH)
+    pl.semaphore_wait(barrier, n)
 
     def remote(src, dst, send, recv, target):
         return pltpu.make_async_remote_copy(
@@ -126,18 +134,21 @@
             codes_ref.at[target], codes_in.at[me], code_send.at[k], code_recv.at[k], target
         )
 
+    def stride(k):
+        return lax.rem(me + lax.rem(k * (n // 2 - 1), n), n)
+
     def rand(k):
-        target = lax.rem(me + k, n)
+        target = stride(k)
         return remote(
             stage.at[pl.ds(target * cap, cap)], arr.at[pl.ds(me * cap, cap)],
             rand_send.at[k], rand_recv.at[k], target,
         )
 
-    def each(body):
+    def each(body, first=1, last=n):
         def step(k, c):
             body(k)
             return c
-        lax.fori_loop(1, n, step, 0)
+        lax.fori_loop(first, last, step, 0)
 
     each(lambda k: code(k).start())
     codes_in[pl.ds(me, 1)] = codes_ref[pl.ds(me, 1)]
@@ -149,7 +160,7 @@
     tail = (blocks - 1) * block_len
     up, down = lax.rem(me + 1, n), lax.rem(me + n - 1, n)
     edges = []
-    for i, ref in enumerate((k_ref, v_ref)):
+    for i, ref in enumerate((k_hbm, v_hbm)):
         edges.append(remote(
             ref.at[tail : tail + block_len], low.at[i], edge_send.at[0, i], edge_recv.at[0, i], up
         ))
@@ -159,6 +170,8 @@
     for copy in edges:
         copy.start()
 
+    for copy in loads:
+        copy.wait()
     for b in range(blocks):
         rows = slice(b * block_len, (b + 1) * block_len)
         for h in range(heads):
@@ -166,24 +179,56 @@
             pairs[b * heads + h, :, 0:head_dim] = k_ref[rows, cols]
             pairs[b * heads + h, :, head_dim:wide] = v_ref[rows, cols]
 
-    def candidate(block, out, lead):
+    plane = 2 * y + x
+    mates = ((0, 1), (1, 0), (1, 1))
+
+    def mate(dy, dx):
+        return lax.rem(y + dy, 2), lax.rem(x + dx, 2)
+
+    def plane_cut(i):
+        ty, tx = mate(*mates[i])
+        return remote(
+            cand.at[tx, pl.ds(ty * part, part)], got_p.at[plane], cut_send.at[i], cut_recv.at[i],
+            z * 4 + ty * 2 + tx,
+        )
+
+    def line_give(dz):
+        to = lax.rem(z + dz, lines)
+        return remote(got_z.at[z], got_z.at[z], line_out.at[dz], line_in.at[dz], to * 4 + plane)
+
+    def plane_give(i):
+        ty, tx = mate(*mates[i])
+        piece = shared.at[x, pl.ds(y * part, part)]
+        return remote(piece, piece, give_send.at[i], give_recv.at[i], z * 4 + ty * 2 + tx)
+
+    for g in range(2):
+        base = glob_ref[g] % blocks * heads
         for h in range(heads):
-            pair = pairs[block % blocks * heads + h]
-            for r in range(tiles):
-                rows = slice(r * TILE, (r + 1) * TILE)
-                out[(*lead, 0, h * tiles + r)] = pair[rows, 0:head_dim]
-                out[(*lead, 1, h * tiles + r)] = pair[rows, head_dim:wide]
-
-    away = glob_ref[1 - x]
-    candidate(away, send_x, ())
-    glob_x = remote(send_x, pair_x.at[1], glob_send.at[0], glob_recv.at[0], other_x)
-    glob_x.start()
-    mine = glob_ref[x]
-    candidate(mine, pair_x, (0,))
-    holder = mine // blocks
-    pick_x = lax.rem(holder + x, 2)
-    pick_y = lax.rem(holder // 2 + y, 2)
-    pick_z = holder // 4
+            cand[g, h] = pairs[base + h]
+    for i in range(3):
+        plane_cut(i).start()
+    got_p[plane] = cand[x, pl.ds(y * part, part)]
+    holder = glob_ref[x] // blocks
+
+    def globals_line():
+        for i in range(3):
+            plane_cut(i).wait_recv()
+        got_z[z] = got_p[holder % 4]
+        for dz in range(1, lines):
+            line_give(dz).start()
+
+    def globals_plane():
+        for dz in range(1, lines):
+            line_give(dz).wait_recv()
+        shared[x, pl.ds(y * part, part)] = got_z[holder // 4]
+        for i in range(3):
+            plane_give(i).start()
+
+    def globals_done():
+        for i in range(3):
+            plane_give(i).wait_recv()
+        for copy in edges:
+            copy.wait_recv()
 
     each(lambda k: code(k).wait_recv())
     to_smem = pltpu.make_async_copy(codes_in, codes, local.at[1])
@@ -195,75 +240,16 @@
             out[place * cap + s] = pairs[codes[target, 0, s]]
 
     def ship(k):
-        target = lax.rem(me + k, n)
+        target = stride(k)
         pack(target, stage, target)
         rand(k).start()
-
-    each(ship)
-    pack(me, arr, me)
-
-    glob_x.wait_recv()
-    picked = pair_x.at[:, 1 - y]
-    send_y[...] = picked[pick_x]
-    glob_y = remote(send_y, pair_y.at[1], glob_send.at[1], glob_recv.at[1], other_y)
-    glob_y.start()
-    picked = pair_x.at[:, y]
-    pair_y[0] = picked[pick_x]
-
-    advance(1)
-
-    def line(dz):
-        return lax.rem(z + dz, lines)
-
-    def zcut(dz):
-        to = line(dz)
-        return remote(
-            cut_z.at[pl.ds(to * share, share)], got_z.at[z], zcut_send.at[dz], zcut_recv.at[dz],
-            to * 4 + y * 2 + x,
-        )
-
-    def zgive(dz):
-        piece = shared.at[x, y, pl.ds(z * share, share)]
-        return remote(
-            piece, piece, zgive_send.at[dz], zgive_recv.at[dz], line(dz) * 4 + y * 2 + x
-        )
-
-    glob_y.wait_recv()
-    cut_z[...] = pair_y[pick_y]
-    for dz in range(1, lines):
-        zcut(dz).start()
-    got_z[z] = cut_z[pl.ds(z * share, share)]
-
-    forward(0)
-
-    for dz in range(1, lines):
-        zcut(dz).wait_recv()
-    shared[x, y, pl.ds(z * share, share)] = got_z[pick_z]
-    for dz in range(1, lines):
-        zgive(dz).start()
-    for dz in range(1, lines):
-        zgive(dz).wait_recv()
-    give_y = remote(
-        shared.at[x, y], shared.at[x, y], glob_send.at[2], glob_recv.at[2], other_y
-    )
-    give_y.start()
-    give_y.wait_recv()
-    give_x = remote(shared.at[x], shared.at[x], glob_send.at[3], glob_recv.at[3], other_x)
-    give_x.start()
-
-    if lines > 2:
-        advance(2)
-    give_x.wait_recv()
-    for copy in edges:
-        copy.wait_recv()
 
     def begin(h, c):
         cols = pl.ds(pl.multiple_of(h * head_dim, head_dim), head_dim)
         kk = jnp.concatenate([low[0, :, cols], k_ref[:, cols], high[0, :, cols]], axis=0)
         vv = jnp.concatenate([low[1, :, cols], v_ref[:, cols], high[1, :, cols]], axis=0)
-        chunk = pl.ds(h * tiles, tiles)
-        kg = [shared[i, 0, chunk].reshape(block_len, head_dim) for i in range(2)]
-        vg = [shared[i, 1, chunk].reshape(block_len, head_dim) for i in range(2)]
+        kg = [shared[i, h, :, 0:head_dim] for i in range(2)]
+        vg = [shared[i, h, :, head_dim:wide] for i in range(2)]
         for b in range(blocks):
             lo, hi = b * block_len, (b + 3) * block_len
             ks = jnp.concatenate([kk[lo:hi], *kg], axis=0)
@@ -302,21 +288,78 @@
             o = acc[rows, cols] * fade + jnp.dot(
                 expo.astype(jnp.bfloat16), vr, preferred_element_type=jnp.float32
             )
-            o_ref[rows, cols] = (o * (1.0 / total)).astype(o_ref.dtype)
+            att[rows, cols] = (o * (1.0 / total)).astype(att.dtype)
         return c
 
-    steps = [functools.partial(forward, 1)]
+    def attend(h0, h1):
+        lax.fori_loop(h0, h1, begin, 0)
+
+    third = n // 3
+    each(ship, 1, 4)
+    globals_line()
+    advance(1)
+    globals_plane()
+    each(ship, 4, 8)
+    forward(0)
+    if lines > 2:
+        advance(2)
+    each(ship, 8, n)
+    pack(me, arr, me)
+    forward(1)
+    globals_done()
+    attend(0, 2)
     for t in range(3, lines):
-        steps += [functools.partial(advance, t), functools.partial(forward, t - 1)]
-    cutoffs = [heads * i // len(steps) for i in range(len(steps) + 1)]
-    for step, h0, h1 in zip(steps, cutoffs, cutoffs[1:]):
-        if h1 > h0:
-            lax.fori_loop(h0, h1, begin, 0)
-        step()
+        advance(t)
+        if t == 3:
+            attend(2, 4)
+        forward(t - 1)
+    attend(4, 6)
     forward(lines - 1)
+    attend(6, heads)
 
     each(lambda k: rand(k).wait_recv())
     lax.fori_loop(0, heads, finish, 0)
+
+    for t in range(lines):
+        for side in sides(t):
+            @pl.when(exists(side, t))
+            def _():
+                for way in (0, 1):
+                    far(side, t, way).wait_recv()
+    own_rows.wait()
+
+    kept = out_ref.shape[0]
+    depth = full_ref.shape[0] * full_ref.shape[1]
+    step = give.shape[2]
+    chunks = give.shape[0]
+
+    def product(row, c):
+        cols = pl.ds(pl.multiple_of(c * step, step), step)
+        return jnp.dot(
+            att[pl.ds(pl.multiple_of(row, kept), kept)],
+            full_ref[:, :, cols].reshape(depth, step),
+            preferred_element_type=jnp.float32,
+        )
+
+    def hand(c):
+        return pltpu.make_async_remote_copy(
+            src_ref=give.at[c], dst_ref=take.at[c], send_sem=core_send.at[c],
+            recv_sem=core_recv.at[c], device_id={"head": 1 - hd}, device_id_type=MESH,
+        )
+
+    def theirs(c):
+        give[c] = product((1 - hd) * kept, c).astype(give.dtype)
+        hand(c).start()
+
+    def ours(c):
+        mine = product(hd * kept, c).astype(give.dtype).astype(jnp.float32)
+        hand(c).wait_recv()
+        cols = pl.ds(pl.multiple_of(c * step, step), step)
+        out_ref[:, cols] = (mine + take[c].astype(jnp.float32)).astype(out_ref.dtype)
+
+    each(theirs, 0, chunks)
+    each(ours, 0, chunks)
+    each(lambda c: hand(c).wait_send(), 0, chunks)
 
     for t in range(lines):
         for side in (0, 1):
@@ -329,22 +372,22 @@
             def _():
                 for way in (0, 1):
                     near(side, t, way).wait_send()
-                    far(side, t, way).wait()
+                    far(side, t, way).wait_send()
     each(lambda k: code(k).wait_send())
     each(lambda k: rand(k).wait_send())
+    for i in range(3):
+        plane_cut(i).wait_send()
+        plane_give(i).wait_send()
     for dz in range(1, lines):
-        zcut(dz).wait_send()
-        zgive(dz).wait_send()
-    for copy in (glob_x, glob_y, give_y, give_x, *edges):
+        line_give(dz).wait_send()
+    for copy in edges:
         copy.wait_send()
-    own_rows.wait()
 
 
 def layer(glob, places, codes, q, k, v, weight, n, cap, blocks, block_len, head_dim, heads):
     lines = n // 4
     rows, columns = weight.shape
     tokens, width = q.shape
-    tiles = heads * block_len // TILE
     dma = pltpu.SemaphoreType.DMA
     vmem = pl.BlockSpec(memory_space=pltpu.VMEM)
     smem = pl.BlockSpec(memory_space=pltpu.SMEM)
@@ -352,18 +395,23 @@
     kind = q.dtype
     f32 = jnp.float32
     slots = (n * cap, block_len, 2 * head_dim)
-    tile = (TILE, LANES)
+    pair = (block_len, 2 * head_dim)
+    chunks = 8
     return pl.pallas_call(
         functools.partial(
             layer_kernel, n, cap, blocks, block_len, head_dim, heads, head_dim ** (-0.5)
         ),
-        out_shape=(
-            jax.ShapeDtypeStruct((n, rows, columns), kind),
-            jax.ShapeDtypeStruct((tokens, width), kind),
-        ),
-        in_specs=[smem, smem, vmem, vmem, vmem, vmem, vmem],
-        out_specs=(hbm, vmem),
+        out_shape=jax.ShapeDtypeStruct((tokens // 2, columns), kind),
+        in_specs=[smem, smem, vmem, hbm, hbm, hbm, hbm],
+        out_specs=vmem,
         scratch_shapes=[
+            pltpu.VMEM(q.shape, kind),
+            pltpu.VMEM(q.shape, kind),
+            pltpu.VMEM(q.shape, kind),
+            pltpu.VMEM((n, rows, columns), kind),
+            pltpu.VMEM(q.shape, kind),
+            pltpu.VMEM((chunks, tokens // 2, columns // chunks), kind),
+            pltpu.VMEM((chunks, tokens // 2, columns // chunks), kind),
             pltpu.VMEM((blocks * heads, block_len, 2 * head_dim), kind),
             pltpu.VMEM(slots, kind),
             pltpu.VMEM(slots, kind),
@@ -371,13 +419,10 @@
             pltpu.SMEM(codes.shape, jnp.int32),
             pltpu.VMEM((2, block_len, width), kind),
             pltpu.VMEM((2, block_len, width), kind),
-            pltpu.VMEM((2, 2, tiles, *tile), kind),
-            pltpu.VMEM((2, tiles, *tile), kind),
-            pltpu.VMEM((2, tiles, *tile), kind),
-            pltpu.VMEM((tiles, *tile), kind),
-            pltpu.VMEM((tiles, *tile), kind),
-            pltpu.VMEM((lines, tiles // lines, *tile), kind),
-            pltpu.VMEM((2, 2, tiles, *tile), kind),
+            pltpu.VMEM((2, heads, *pair), kind),
+            pltpu.VMEM((4, heads // 2, *pair), kind),
+            pltpu.VMEM((lines, heads // 2, *pair), kind),
+            pltpu.VMEM((2, heads, *pair), kind),
             pltpu.VMEM((tokens, width), f32),
             pltpu.VMEM((heads, tokens, LANES), f32),
             pltpu.VMEM((heads, tokens, LANES), f32),
@@ -386,12 +431,11 @@
             dma((2, lines, 2)), dma((2, lines, 2)),
             dma((n,)), dma((n,)), dma((n,)), dma((n,)),
             dma((2, 2)), dma((2, 2)),
-            dma((4,)), dma((4,)),
-            dma((lines,)), dma((lines,)), dma((lines,)), dma((lines,)),
-            dma((2,)),
+            dma((3,)), dma((3,)), dma((lines,)), dma((lines,)), dma((3,)), dma((3,)),
+            dma((chunks,)), dma((chunks,)), dma((5,)),
         ],
         compiler_params=pltpu.CompilerParams(
-            collective_id=0, has_side_effects=True, vmem_limit_bytes=48 << 20
+            collective_id=0, has_side_effects=True, vmem_limit_bytes=60 << 20
         ),
         cost_estimate=pl.CostEstimate(
             flops=4 * tokens * 6 * block_len * width,
@@ -403,7 +447,6 @@
 
 
 def body(queries, keys, values, rand_blocks, global_blocks, out_weight):
-    f32 = jnp.float32
     n = lax.axis_size("seq")
     block_count, head_count = rand_blocks.shape
     tokens, width = queries.shape
@@ -422,14 +465,9 @@
     hits = (owners[None, None, :] == target) & (ranks[None, None, :] == slot)
     outgoing = jnp.sum(jnp.where(hits, codes[None, None, :], 0), axis=2)
 
-    group_rows, attended = layer(
+    return layer(
         global_blocks, owners * cap + ranks, outgoing.reshape(n, 1, LANES), queries, keys, values,
         out_weight, n, cap, block_count, block_len, head_dim, head_count,
-    )
-    group_rows = group_rows.reshape(n * out_weight.shape[0], out_weight.shape[1])
-    partial_value = jnp.dot(attended, group_rows, preferred_element_type=f32)
-    return lax.psum_scatter(
-        partial_value.astype(jnp.bfloat16), "head", scatter_dimension=0, tiled=True
     )
 
 

time: 243 us -> 192 us (0.79)
  Pallas kernels: 202 us -> 185 us
  between operations: 13.4 us -> 0.02 us
  waiting for transfers between devices: 11.1 us -> 0 us
  matrix products: 9.39 us -> 0 us
    pallas_call x1, Pallas kernels: 202 us -> 185 us  [layer(): pl.pallas_call(functools.partial(layer_kernel, n, cap, blocks, block_len,...]
    reduce_scatter x1 -> x0, waiting for transfers between devices: 11 us -> none  [body(): lax.psum_scatter(partial_value.astype(jnp.bfloat16), 'head', scatter_dime...]
    dot_general x1 -> x0, matrix products: 9.39 us -> none  [body(): partial_value = jnp.dot(attended, group_rows, preferred_element_type=f32)]
    unnamed x10 -> x1, local copies, waits for them, and re-layouts: 5.36 us -> 3.13 us
  transfers between devices with their start and end apart: 1 -> 0, of which waited for: 1 -> 0; matrix products, arithmetic and copies ran while one was open for 0% -> 0% of each run, Pallas kernels for 0% -> 0%
where the time goes in v2:
time: 192 us; the launch traced here: 191 us
  Pallas kernels  185 us (96%)
  local copies, waits for them, and re-layouts  3.89 us (2%)
    pallas_call x1, Pallas kernels, layer(): pl.pallas_call(functools.partial(layer_kernel, n, cap, blocks, block_len,...  185 us

profile of v2, /device:TPU:0, one launch (start us, length us, event | category | flops | bytes accessed | tf_op | source)
XLA Modules:
  0.0 191.0 jit_solution(3752023850444973954)
XLA Ops:
  0.0 0.8 reshape.169
  0.8 0.2 convert_reduce_fusion
  1.0 0.5 multiply_add_fusion.slot_ref
  1.5 0.1 iota_compare_fusion
  1.6 0.8 select_reduce_fusion
  2.4 185.4 %layer.1 = bf16[256,4096]{1,0:T(8,128)(2,1)} custom-call(s32[2]{0:T(128)} %glob_ref.1, s32[64]{0:T(128)} %multiply_add_fusion.slot_ref, s32[16,1,128]{2,1,0:T(1,128)} %bitcast.1, bf16[512,1024]{1,0:T(8,128)(2,1)} %q_hbm.1, bf16[512,1024]{1,0:T(8,128)(2,1)} %k_hbm.1, bf16[512,1024]{1,0:T(8,128)(2,1)} %v_hbm.1, bf16[64,4096]{1,0:T(8,128)(2,1)} %w_ref.1), custom_call_target="tpu_custom_call" | custom-call | flops 805306368 | bytes 167772160 | tf_op jit(solution)/shard_map/layer/pallas_call | solution.py:400
  187.9 3.1 %copy.8 = bf16[256,4096]{1,0:T(8,128)(2,1)} copy(bf16[256,4096]{1,0:T(8,128)(2,1)} %layer.1) | data formatting | bytes 4194304
  (2 shorter events, 0.0 us)

commit v3 on v2

--- a/solution.py
+++ b/solution.py
@@ -250,45 +250,62 @@
         vv = jnp.concatenate([low[1, :, cols], v_ref[:, cols], high[1, :, cols]], axis=0)
         kg = [shared[i, h, :, 0:head_dim] for i in range(2)]
         vg = [shared[i, h, :, head_dim:wide] for i in range(2)]
-        for b in range(blocks):
-            lo, hi = b * block_len, (b + 3) * block_len
-            ks = jnp.concatenate([kk[lo:hi], *kg], axis=0)
-            vs = jnp.concatenate([vv[lo:hi], *vg], axis=0)
-            s = lax.dot_general(
-                q_ref[lo : lo + block_len, cols], ks, (((1,), (1,)), ((), ())),
-                preferred_element_type=jnp.float32,
-            ) * scale
-            top = jnp.max(s, axis=-1, keepdims=True)
-            expo = jnp.exp(s - top)
-            total = jnp.sum(expo, axis=-1, keepdims=True)
-            rows = pl.ds(lo, block_len)
-            acc[rows, cols] = jnp.dot(
-                expo.astype(jnp.bfloat16), vs, preferred_element_type=jnp.float32
+        kg, vg = jnp.concatenate(kg, axis=0), jnp.concatenate(vg, axis=0)
+        q = q_ref[:, cols]
+
+        def against(rows, table):
+            return lax.dot_general(
+                rows, table, (((1,), (1,)), ((), ())), preferred_element_type=jnp.float32
             )
-            top_s[h, rows] = jnp.broadcast_to(top, (block_len, LANES))
-            sum_s[h, rows] = jnp.broadcast_to(total, (block_len, LANES))
+
+        def rows_of(array, b, count=1):
+            return array[b * block_len : (b + count) * block_len]
+
+        near_s = jnp.concatenate(
+            [against(rows_of(q, b), rows_of(kk, b, 3)) for b in range(blocks)], axis=0
+        ) * scale
+        glob_s = against(q, kg) * scale
+        top = jnp.maximum(
+            jnp.max(near_s, axis=-1, keepdims=True), jnp.max(glob_s, axis=-1, keepdims=True)
+        )
+        near_e, glob_e = jnp.exp(near_s - top), jnp.exp(glob_s - top)
+        total = jnp.sum(near_e, axis=-1, keepdims=True) + jnp.sum(glob_e, axis=-1, keepdims=True)
+        near_w = near_e.astype(jnp.bfloat16)
+        o = jnp.concatenate([
+            jnp.dot(rows_of(near_w, b), rows_of(vv, b, 3), preferred_element_type=jnp.float32)
+            for b in range(blocks)
+        ], axis=0)
+        acc[:, cols] = o + jnp.dot(
+            glob_e.astype(jnp.bfloat16), vg, preferred_element_type=jnp.float32
+        )
+        top_s[h] = jnp.broadcast_to(top, top_s.shape[1:])
+        sum_s[h] = jnp.broadcast_to(total, sum_s.shape[1:])
         return c
 
     def finish(h, c):
         cols = pl.ds(pl.multiple_of(h * head_dim, head_dim), head_dim)
-        for b in range(blocks):
-            e = b * heads + h
-            pair = arr[slot_ref[e]]
-            kr, vr = pair[:, 0:head_dim], pair[:, head_dim:wide]
-            rows = pl.ds(b * block_len, block_len)
-            s = lax.dot_general(
-                q_ref[rows, cols], kr, (((1,), (1,)), ((), ())),
+        picked = [arr[slot_ref[b * heads + h]] for b in range(blocks)]
+        s = jnp.concatenate([
+            lax.dot_general(
+                q_ref[b * block_len : (b + 1) * block_len, cols], pair[:, 0:head_dim],
+                (((1,), (1,)), ((), ())), preferred_element_type=jnp.float32,
+            )
+            for b, pair in enumerate(picked)
+        ], axis=0) * scale
+        before = top_s[h]
+        top = jnp.maximum(before, jnp.max(s, axis=-1, keepdims=True))
+        fade = jnp.exp(before - top)
+        expo = jnp.exp(s - top[:, 0:block_len])
+        total = sum_s[h] * fade + jnp.sum(expo, axis=-1, keepdims=True)
+        weight = expo.astype(jnp.bfloat16)
+        o = jnp.concatenate([
+            jnp.dot(
+                weight[b * block_len : (b + 1) * block_len], pair[:, head_dim:wide],
                 preferred_element_type=jnp.float32,
-            ) * scale
-            before = top_s[h, rows, 0:1]
-            top = jnp.maximum(before, jnp.max(s, axis=-1, keepdims=True))
-            fade = jnp.exp(before - top)
-            expo = jnp.exp(s - top)
-            total = sum_s[h, rows, 0:1] * fade + jnp.sum(expo, axis=-1, keepdims=True)
-            o = acc[rows, cols] * fade + jnp.dot(
-                expo.astype(jnp.bfloat16), vr, preferred_element_type=jnp.float32
             )
-            att[rows, cols] = (o * (1.0 / total)).astype(att.dtype)
+            for b, pair in enumerate(picked)
+        ], axis=0)
+        att[:, cols] = ((acc[:, cols] * fade + o) * (1.0 / total)).astype(att.dtype)
         return c
 
     def attend(h0, h1):

time: 192 us -> 174 us (0.906)
  Pallas kernels: 185 us -> 167 us
    pallas_call x1, Pallas kernels: 185 us -> 167 us  [layer(): pl.pallas_call(functools.partial(layer_kernel, n, cap, blocks, block_len,...]
where the time goes in v3:
time: 174 us; the launch traced here: 173 us
  Pallas kernels  167 us (96%)
  local copies, waits for them, and re-layouts  3.89 us (2%)
    pallas_call x1, Pallas kernels, layer(): pl.pallas_call(functools.partial(layer_kernel, n, cap, blocks, block_len,...  167 us

profile of v3, /device:TPU:0, one launch (start us, length us, event | category | flops | bytes accessed | tf_op | source)
XLA Modules:
  0.0 172.5 jit_solution(13346355705067092604)
XLA Ops:
  0.0 0.8 reshape.169
  0.8 0.2 convert_reduce_fusion
  1.0 0.5 multiply_add_fusion.slot_ref
  1.5 0.1 iota_compare_fusion
  1.6 0.8 select_reduce_fusion
  2.4 166.9 %layer.1 = bf16[256,4096]{1,0:T(8,128)(2,1)} custom-call(s32[2]{0:T(128)} %glob_ref.1, s32[64]{0:T(128)} %multiply_add_fusion.slot_ref, s32[16,1,128]{2,1,0:T(1,128)} %bitcast.1, bf16[512,1024]{1,0:T(8,128)(2,1)} %q_hbm.1, bf16[512,1024]{1,0:T(8,128)(2,1)} %k_hbm.1, bf16[512,1024]{1,0:T(8,128)(2,1)} %v_hbm.1, bf16[64,4096]{1,0:T(8,128)(2,1)} %w_ref.1), custom_call_target="tpu_custom_call" | custom-call | flops 805306368 | bytes 167772160 | tf_op jit(solution)/shard_map/layer/pallas_call | solution.py:417
  169.4 3.1 %copy.8 = bf16[256,4096]{1,0:T(8,128)(2,1)} copy(bf16[256,4096]{1,0:T(8,128)(2,1)} %layer.1) | data formatting | bytes 4194304
  (2 shorter events, 0.0 us)

commit v4 on v3

--- a/solution.py
+++ b/solution.py
@@ -311,28 +311,25 @@
     def attend(h0, h1):
         lax.fori_loop(h0, h1, begin, 0)
 
-    third = n // 3
-    each(ship, 1, 4)
+    each(ship, 1, n // 4)
+    advance(1)
     globals_line()
-    advance(1)
-    globals_plane()
-    each(ship, 4, 8)
+    each(ship, n // 4, n // 2)
     forward(0)
     if lines > 2:
         advance(2)
-    each(ship, 8, n)
+    globals_plane()
+    each(ship, n // 2, n)
     pack(me, arr, me)
     forward(1)
-    globals_done()
-    attend(0, 2)
     for t in range(3, lines):
         advance(t)
         if t == 3:
-            attend(2, 4)
+            globals_done()
         forward(t - 1)
-    attend(4, 6)
+    attend(0, heads // 2)
     forward(lines - 1)
-    attend(6, heads)
+    attend(heads // 2, heads)
 
     each(lambda k: rand(k).wait_recv())
     lax.fori_loop(0, heads, finish, 0)

time: 174 us -> 164 us (0.943); the launches traced: 173 us -> 161 us
  Pallas kernels: 167 us -> 155 us
    pallas_call x1, Pallas kernels: 167 us -> 155 us  [layer(): pl.pallas_call(functools.partial(layer_kernel, n, cap, blocks, block_len,...]
where the time goes in v4:
time: 164 us; the launch traced here: 161 us
  Pallas kernels  155 us (95%)
  local copies, waits for them, and re-layouts  3.89 us (2%)
    pallas_call x1, Pallas kernels, layer(): pl.pallas_call(functools.partial(layer_kernel, n, cap, blocks, block_len,...  155 us

profile of v4, /device:TPU:0, one launch (start us, length us, event | category | flops | bytes accessed | tf_op | source)
XLA Modules:
  0.0 160.5 jit_solution(16998923692299924312)
XLA Ops:
  0.0 0.8 reshape.169
  0.8 0.2 convert_reduce_fusion
  1.0 0.5 multiply_add_fusion.slot_ref
  1.5 0.1 iota_compare_fusion
  1.6 0.8 select_reduce_fusion
  2.4 155.0 %layer.1 = bf16[256,4096]{1,0:T(8,128)(2,1)} custom-call(s32[2]{0:T(128)} %glob_ref.1, s32[64]{0:T(128)} %multiply_add_fusion.slot_ref, s32[16,1,128]{2,1,0:T(1,128)} %bitcast.1, bf16[512,1024]{1,0:T(8,128)(2,1)} %q_hbm.1, bf16[512,1024]{1,0:T(8,128)(2,1)} %k_hbm.1, bf16[512,1024]{1,0:T(8,128)(2,1)} %v_hbm.1, bf16[64,4096]{1,0:T(8,128)(2,1)} %w_ref.1), custom_call_target="tpu_custom_call" | custom-call | flops 805306368 | bytes 167772160 | tf_op jit(solution)/shard_map/layer/pallas_call | solution.py:414
  157.4 3.1 %copy.8 = bf16[256,4096]{1,0:T(8,128)(2,1)} copy(bf16[256,4096]{1,0:T(8,128)(2,1)} %layer.1) | data formatting | bytes 4194304
  (2 shorter events, 0.0 us)

commit v5 on v4

--- a/solution.py
+++ b/solution.py
@@ -410,7 +410,7 @@
     f32 = jnp.float32
     slots = (n * cap, block_len, 2 * head_dim)
     pair = (block_len, 2 * head_dim)
-    chunks = 8
+    chunks = 4
     return pl.pallas_call(
         functools.partial(
             layer_kernel, n, cap, blocks, block_len, head_dim, heads, head_dim ** (-0.5)

time: 164 us -> 162 us (0.988)
  Pallas kernels: 155 us -> 153 us
where the time goes in v5:
time: 162 us; the launch traced here: 159 us
  Pallas kernels  153 us (94%)
  local copies, waits for them, and re-layouts  3.89 us (2%)
  other arithmetic  1.64 us (1%)
    pallas_call x1, Pallas kernels, layer(): pl.pallas_call(functools.partial(layer_kernel, n, cap, blocks, block_len,...  153 us

profile of v5, /device:TPU:0, one launch (start us, length us, event | category | flops | bytes accessed | tf_op | source)
XLA Modules:
  0.0 159.0 jit_solution(15323976784902440569)
XLA Ops:
  0.0 0.8 reshape.169
  0.8 0.2 convert_reduce_fusion
  1.0 0.5 multiply_add_fusion.slot_ref
  1.5 0.1 iota_compare_fusion
  1.6 0.8 select_reduce_fusion
  2.4 153.5 %layer.1 = bf16[256,4096]{1,0:T(8,128)(2,1)} custom-call(s32[2]{0:T(128)} %glob_ref.1, s32[64]{0:T(128)} %multiply_add_fusion.slot_ref, s32[16,1,128]{2,1,0:T(1,128)} %bitcast.1, bf16[512,1024]{1,0:T(8,128)(2,1)} %q_hbm.1, bf16[512,1024]{1,0:T(8,128)(2,1)} %k_hbm.1, bf16[512,1024]{1,0:T(8,128)(2,1)} %v_hbm.1, bf16[64,4096]{1,0:T(8,128)(2,1)} %w_ref.1), custom_call_target="tpu_custom_call" | custom-call | flops 805306368 | bytes 167772160 | tf_op jit(solution)/shard_map/layer/pallas_call | solution.py:414
  155.9 3.1 %copy.8 = bf16[256,4096]{1,0:T(8,128)(2,1)} copy(bf16[256,4096]{1,0:T(8,128)(2,1)} %layer.1) | data formatting | bytes 4194304
  (2 shorter events, 0.0 us)

commit v6 on v5

--- a/solution.py
+++ b/solution.py
@@ -11,19 +11,12 @@
 LANES = 128
 
 
-def ranked(owners):
-    count = owners.shape[0]
-    order = jnp.arange(count, dtype=jnp.int32)
-    earlier = (owners[:, None] == owners[None, :]) & (order[None, :] < order[:, None])
-    return jnp.sum(earlier.astype(jnp.int32), axis=1)
-
-
 def layer_kernel(
     n, cap, blocks, block_len, head_dim, heads, scale,
-    glob_ref, slot_ref, codes_ref, q_hbm, k_hbm, v_hbm, w_ref,
+    glob_ref, rand_ref, q_hbm, k_hbm, v_hbm, w_ref,
     out_ref,
     q_ref, k_ref, v_ref, full_ref, att, give, take,
-    pairs, stage, arr, codes_in, codes, low, high, cand, got_p, got_z, shared,
+    slot_row, slot_ref, codes_ref, pairs, stage, arr, codes_in, codes, low, high, cand, got_p, got_z, shared,
     acc, top_s, sum_s,
     line_send, line_recv, near_send, near_recv, far_send, far_recv,
     code_send, code_recv, rand_send, rand_recv, edge_send, edge_recv,
@@ -56,6 +49,29 @@
 
     lax.fori_loop(1, n, greet, 0)
     pl.semaphore_signal(barrier, inc=1, device_id={"head": 1 - hd}, device_id_type=MESH)
+
+    def named(e):
+        return rand_ref[lax.div(e, heads), lax.rem(e, heads)]
+
+    owner_of = lax.broadcasted_iota(jnp.int32, (n, LANES), 0)
+    slot_of = lax.broadcasted_iota(jnp.int32, (n, LANES), 1)
+
+    def enlist(e, c):
+        seen, table, places = c
+        block = named(e)
+        asked = owner_of == lax.div(block, blocks)
+        entry = lax.rem(block, blocks) * heads + lax.rem(e, heads)
+        table = jnp.where(asked & (slot_of == seen), entry, table)
+        places = jnp.where(asked & (slot_of == e), owner_of * cap + seen, places)
+        return jnp.where(asked, seen + 1, seen), table, places
+
+    zeros = jnp.zeros((n, LANES), jnp.int32)
+    _, table, places = lax.fori_loop(0, blocks * heads, enlist, (zeros, zeros, zeros))
+    slot_row[...] = jnp.sum(places, axis=0, keepdims=True)
+    slots_down = pltpu.make_async_copy(slot_row, slot_ref, local.at[5])
+    slots_down.start()
+    for t in range(n):
+        codes_ref[t] = table[t : t + 1]
     pl.semaphore_wait(barrier, n)
 
     def remote(src, dst, send, recv, target):
@@ -284,7 +300,7 @@
 
     def finish(h, c):
         cols = pl.ds(pl.multiple_of(h * head_dim, head_dim), head_dim)
-        picked = [arr[slot_ref[b * heads + h]] for b in range(blocks)]
+        picked = [arr[slot_ref[0, b * heads + h]] for b in range(blocks)]
         s = jnp.concatenate([
             lax.dot_general(
                 q_ref[b * block_len : (b + 1) * block_len, cols], pair[:, 0:head_dim],
@@ -330,6 +346,7 @@
     attend(0, heads // 2)
     forward(lines - 1)
     attend(heads // 2, heads)
+    slots_down.wait()
 
     each(lambda k: rand(k).wait_recv())
     lax.fori_loop(0, heads, finish, 0)
@@ -398,8 +415,9 @@
         copy.wait_send()
 
 
-def layer(glob, places, codes, q, k, v, weight, n, cap, blocks, block_len, head_dim, heads):
+def layer(glob, rand, q, k, v, weight, n, cap, blocks, block_len, head_dim, heads):
     lines = n // 4
+    codes = (n, 1, LANES)
     rows, columns = weight.shape
     tokens, width = q.shape
     dma = pltpu.SemaphoreType.DMA
@@ -416,7 +434,7 @@
             layer_kernel, n, cap, blocks, block_len, head_dim, heads, head_dim ** (-0.5)
         ),
         out_shape=jax.ShapeDtypeStruct((tokens // 2, columns), kind),
-        in_specs=[smem, smem, vmem, hbm, hbm, hbm, hbm],
+        in_specs=[smem, smem, hbm, hbm, hbm, hbm],
         out_specs=vmem,
         scratch_shapes=[
             pltpu.VMEM(q.shape, kind),
@@ -426,11 +444,14 @@
             pltpu.VMEM(q.shape, kind),
             pltpu.VMEM((chunks, tokens // 2, columns // chunks), kind),
             pltpu.VMEM((chunks, tokens // 2, columns // chunks), kind),
+            pltpu.VMEM((1, LANES), jnp.int32),
+            pltpu.SMEM((1, LANES), jnp.int32),
+            pltpu.VMEM(codes, jnp.int32),
             pltpu.VMEM((blocks * heads, block_len, 2 * head_dim), kind),
             pltpu.VMEM(slots, kind),
             pltpu.VMEM(slots, kind),
-            pltpu.VMEM(codes.shape, jnp.int32),
-            pltpu.SMEM(codes.shape, jnp.int32),
+            pltpu.VMEM(codes, jnp.int32),
+            pltpu.SMEM(codes, jnp.int32),
             pltpu.VMEM((2, block_len, width), kind),
             pltpu.VMEM((2, block_len, width), kind),
             pltpu.VMEM((2, heads, *pair), kind),
@@ -446,7 +467,7 @@
             dma((n,)), dma((n,)), dma((n,)), dma((n,)),
             dma((2, 2)), dma((2, 2)),
             dma((3,)), dma((3,)), dma((lines,)), dma((lines,)), dma((3,)), dma((3,)),
-            dma((chunks,)), dma((chunks,)), dma((5,)),
+            dma((chunks,)), dma((chunks,)), dma((6,)),
         ],
         compiler_params=pltpu.CompilerParams(
             collective_id=0, has_side_effects=True, vmem_limit_bytes=60 << 20
@@ -457,7 +478,7 @@
             bytes_accessed=40 * n * rows * columns,
         ),
         name="layer",
-    )(glob, places, codes, q, k, v, weight)
+    )(glob, rand, q, k, v, weight)
 
 
 def body(queries, keys, values, rand_blocks, global_blocks, out_weight):
@@ -469,19 +490,9 @@
     entries = block_count * head_count
     cap = max(2, (2 * entries + n - 1) // n)
 
-    flat_blocks = rand_blocks.reshape(entries)
-    owners = flat_blocks // block_count
-    head_iota = jnp.arange(entries, dtype=jnp.int32) % head_count
-    codes = flat_blocks % block_count * head_count + head_iota
-    ranks = ranked(owners)
-    target = jnp.arange(n, dtype=jnp.int32)[:, None, None]
-    slot = jnp.arange(LANES, dtype=jnp.int32)[None, :, None]
-    hits = (owners[None, None, :] == target) & (ranks[None, None, :] == slot)
-    outgoing = jnp.sum(jnp.where(hits, codes[None, None, :], 0), axis=2)
-
     return layer(
-        global_blocks, owners * cap + ranks, outgoing.reshape(n, 1, LANES), queries, keys, values,
-        out_weight, n, cap, block_count, block_len, head_dim, head_count,
+        global_blocks, rand_blocks, queries, keys, values, out_weight,
+        n, cap, block_count, block_len, head_dim, head_count,
     )
 
 

time: 162 us -> 160 us (0.988)
  other arithmetic: 1.64 us -> 0 us
where the time goes in v6:
time: 160 us; the launch traced here: 157 us
  Pallas kernels  154 us (96%)
  local copies, waits for them, and re-layouts  3.13 us (2%)
    pallas_call x1, Pallas kernels, layer(): pl.pallas_call(functools.partial(layer_kernel, n, cap, blocks, block_len,...  154 us

profile of v6, /device:TPU:0, one launch (start us, length us, event | category | flops | bytes accessed | tf_op | source)
XLA Modules:
  0.0 156.7 jit_solution(13513645185234850247)
XLA Ops:
  0.0 153.5 %layer.1 = bf16[256,4096]{1,0:T(8,128)(2,1)} custom-call(s32[2]{0:T(128)} %glob_ref.1, s32[8,8]{1,0:T(8,128)} %rand_ref.1, bf16[512,1024]{1,0:T(8,128)(2,1)} %q_hbm.1, bf16[512,1024]{1,0:T(8,128)(2,1)} %k_hbm.1, bf16[512,1024]{1,0:T(8,128)(2,1)} %v_hbm.1, bf16[64,4096]{1,0:T(8,128)(2,1)} %w_ref.1), custom_call_target="tpu_custom_call" | custom-call | flops 805306368 | bytes 167772160 | tf_op jit(solution)/shard_map/layer/pallas_call | solution.py:432
  153.5 3.1 %copy.8 = bf16[256,4096]{1,0:T(8,128)(2,1)} copy(bf16[256,4096]{1,0:T(8,128)(2,1)} %layer.1) | data formatting | bytes 4194304

commit v7 on v6

--- a/solution.py
+++ b/solution.py
@@ -151,7 +151,7 @@
         )
 
     def stride(k):
-        return lax.rem(me + lax.rem(k * (n // 2 - 1), n), n)
+        return lax.rem(me + lax.rem(k * 5, n), n)
 
     def rand(k):
         target = stride(k)

time: 160 us -> 160 us (level)
  no operation moved by 1% of the time
where the time goes in v7:
time: 160 us; the launch traced here: 157 us
  Pallas kernels  154 us (96%)
  local copies, waits for them, and re-layouts  3.13 us (2%)
    pallas_call x1, Pallas kernels, layer(): pl.pallas_call(functools.partial(layer_kernel, n, cap, blocks, block_len,...  154 us

profile of v7, /device:TPU:0, one launch (start us, length us, event | category | flops | bytes accessed | tf_op | source)
XLA Modules:
  0.0 156.7 jit_solution(9941983585982086023)
XLA Ops:
  0.0 153.6 %layer.1 = bf16[256,4096]{1,0:T(8,128)(2,1)} custom-call(s32[2]{0:T(128)} %glob_ref.1, s32[8,8]{1,0:T(8,128)} %rand_ref.1, bf16[512,1024]{1,0:T(8,128)(2,1)} %q_hbm.1, bf16[512,1024]{1,0:T(8,128)(2,1)} %k_hbm.1, bf16[512,1024]{1,0:T(8,128)(2,1)} %v_hbm.1, bf16[64,4096]{1,0:T(8,128)(2,1)} %w_ref.1), custom_call_target="tpu_custom_call" | custom-call | flops 805306368 | bytes 167772160 | tf_op jit(solution)/shard_map/layer/pallas_call | solution.py:432
  153.6 3.1 %copy.8 = bf16[256,4096]{1,0:T(8,128)(2,1)} copy(bf16[256,4096]{1,0:T(8,128)(2,1)} %layer.1) | data formatting | bytes 4194304
